TPU v7x, 512 devices: a whole 4x4x16 slice. The times are simulated.
512 devices in a mesh: lat: 4 (over x_hi, core), lon: 32 (over z, x_lo), tensor: 4 (over y).
Axes of the slice: x: 4 (x_hi: 2, x_lo: 2; x = x_hi * 2 + x_lo), y: 4, z: 16, core: 2. Of those that a mesh axis runs over, the one named last changes fastest.
Arguments:
- fields: bfloat16 [64, 768, 256], P('lat', 'lon'), may hold values from -8 to 8
- norm_gain1: float32 [256], replicated, may hold values from 0.5 to 1.5
- w_qkv: bfloat16 [256, 3, 8, 32], P(None, None, 'tensor'), may hold values from -0.1875 to 0.1875
- logit_scale: float32 [8], P('tensor'), may hold values from 1 to 64
- w_out: bfloat16 [8, 32, 256], P('tensor'), may hold values from -0.375 to 0.375
- attn_keep: int32 [64, 256], P('lat'), may hold values 0 or 1
- dw_kernel: bfloat16 [7, 7, 256], replicated, may hold values from -0.875 to 0.875
- norm_gain2: float32 [256], replicated, may hold values from 0.5 to 1.5
- w_up: bfloat16 [256, 1024], P(None, 'tensor'), may hold values from -0.375 to 0.375
- w_down: bfloat16 [1024, 256], P('tensor'), may hold values from -0.1875 to 0.1875
- mlp_keep: int32 [64, 256], P('lat'), may hold values 0 or 1
Outputs:
- result: bfloat16 [64, 768, 256], P('lat', 'lon')
All inputs are finite; a program needn't handle non-finite values. No bound on the sum of `attn_keep` or of `mlp_keep` on one device may be relied on, other than what follows from the above.
Results may differ from a plain program's by a relative error of at most 0.014.
Values may be sent and summed in bfloat16 or wider, within the bound.
A program may use at most 64 MiB of HBM per device.

v0:
```python
import math
import jax
import jax.numpy as jnp
from jax import lax
from jax.sharding import PartitionSpec as P

ln_eps = 1e-05
keep_prob = 0.9


def padded(shard, sides, width, wrap):
    for axis, dim in sides:
        size, length = (lax.axis_size(axis), shard.shape[dim])
        up = [(i, (i + 1) % size) for i in range(size if wrap else size - 1)]
        down = [(j, i) for i, j in up]
        last = lax.slice_in_dim(shard, length - width, length, axis=dim)
        first = lax.slice_in_dim(shard, 0, width, axis=dim)
        before = lax.ppermute(last, axis, up)
        after = lax.ppermute(first, axis, down)
        shard = jnp.concatenate([before, shard, after], axis=dim)
    return shard


def layer_norm(values, gain):
    widened = values.astype(jnp.float32)
    center = jnp.mean(widened, axis=-1, keepdims=True)
    spread = jnp.mean(jnp.square(widened - center), axis=-1, keepdims=True)
    return (widened - center) * lax.rsqrt(spread + ln_eps) * gain


def depthwise(wide, kernel, rows, cols):
    kernel_f = kernel.astype(jnp.float32)
    wide_f = wide.astype(jnp.float32)
    width = kernel.shape[0]
    total = jnp.zeros((rows, cols, wide.shape[2]), jnp.float32)
    for row_off in range(width):
        for col_off in range(width):
            total = (
                total
                + kernel_f[row_off, col_off]
                * wide_f[row_off : row_off + rows, col_off : col_off + cols]
            )
    return total


def widen(stream, margin):
    rows_wide = padded(stream, (("lat", 0),), margin, False)
    return padded(rows_wide, (("lon", 1),), margin, True)


def feed_forward(spatial, norm_gain2, w_up, w_down):
    normed2 = layer_norm(spatial, norm_gain2).astype(jnp.bfloat16)
    hidden = jax.nn.gelu(
        jnp.einsum("rlc,cf->rlf", normed2, w_up, preferred_element_type=jnp.float32),
        approximate=False,
    ).astype(jnp.bfloat16)
    return jnp.einsum("rlf,fc->rlc", hidden, w_down, preferred_element_type=jnp.float32)


def shards(
    fields,
    norm_gain1,
    w_qkv,
    logit_scale,
    w_out,
    attn_keep,
    dw_kernel,
    norm_gain2,
    w_up,
    w_down,
    mlp_keep,
):
    lat_rows, lon_cols, channels = fields.shape
    local_heads = w_qkv.shape[2]
    head_size = w_qkv.shape[3]
    logit_coef = logit_scale * (1.0 / math.sqrt(head_size))
    normed = layer_norm(fields, norm_gain1).astype(jnp.bfloat16)
    projected = jnp.einsum(
        "rlc,cjhd->rljhd", normed, w_qkv, preferred_element_type=jnp.float32
    ).astype(jnp.bfloat16)
    queries = projected[:, :, 0]
    keys_values = projected[:, :, 1:].reshape(lat_rows, lon_cols, 2 * local_heads * head_size)
    piece = lax.all_gather(keys_values, "lon", axis=1, tiled=True)
    running_max = jnp.full((lat_rows, local_heads, lon_cols), -1e30, jnp.float32)
    count = piece.shape[1]
    split_piece = piece.reshape(lat_rows, count, 2, local_heads, head_size)
    scores = jnp.einsum(
        "rqhd,rkhd->rhqk", queries, split_piece[:, :, 0], preferred_element_type=jnp.float32
    )
    scores = scores * logit_coef[None, :, None, None]
    new_max = jnp.maximum(running_max, jnp.max(scores, axis=-1))
    weights = jnp.exp(scores - new_max[..., None])
    new_sum = jnp.sum(weights, axis=-1)
    gathered = jnp.einsum(
        "rhqk,rkhd->rhqd",
        weights.astype(jnp.bfloat16),
        split_piece[:, :, 1],
        preferred_element_type=jnp.float32,
    )
    mixed = (gathered / new_sum[..., None]).astype(jnp.bfloat16)
    partial_value = jnp.einsum("rhqd,hdc->rqc", mixed, w_out, preferred_element_type=jnp.float32)
    attended = lax.psum(partial_value.astype(jnp.bfloat16), "tensor").astype(jnp.float32)
    attn_factor = (attn_keep.astype(jnp.float32) / keep_prob)[:, None, :]
    mlp_factor = (mlp_keep.astype(jnp.float32) / keep_prob)[:, None, :]
    margin = dw_kernel.shape[0] // 2
    stream = (fields.astype(jnp.float32) + attended * attn_factor).astype(jnp.bfloat16)
    spatial = depthwise(widen(stream, margin), dw_kernel, lat_rows, lon_cols).astype(jnp.bfloat16)
    ffn_sum = lax.psum(
        feed_forward(spatial, norm_gain2, w_up, w_down).astype(jnp.bfloat16), "tensor"
    ).astype(jnp.float32)
    result = (stream.astype(jnp.float32) + ffn_sum * mlp_factor).astype(jnp.bfloat16)
    return result


def solution(mesh):
    placed = (
        P("lat", "lon", None),
        P(),
        P(None, None, "tensor", None),
        P("tensor"),
        P("tensor", None, None),
        P("lat", None),
        P(),
        P(),
        P(None, "tensor"),
        P("tensor", None),
        P("lat", None),
    )
    return jax.shard_map(
        shards, mesh=mesh, in_specs=placed, out_specs=P("lat", "lon", None), check_vma=False
    )
```

profile of v0, /device:TPU:2, one launch (start us, length us, event | category | flops | bytes accessed | tf_op | source)
XLA Modules:
  0.0 309.6 jit_solution(4489916328786344057)
XLA Ops:
  6.5 1.1 convert_reduce_fusion
  7.7 1.2 fusion.18
  8.8 1.4 convolution_convert_fusion
  10.3 0.3 copy.12
  10.6 0.9 reshape.39
  11.5 0.0 all-gather.2.cloned.1.call-update
  11.5 0.0 all-reduce.3.cloned.1.call-start
  11.6 140.8 %all-gather.2.cloned.1.call-done = bf16[16,768,128]{2,1,0:T(8,128)(2,1)} async-done(((bf16[16,24,128]{2,1,0:T(8,128)(2,1)}), bf16[16,768,128]{2,1,0:T(8,128)(2,1)}) %all-gather.2.cloned.1.call-update) | async-done | bytes 3145744 | tf_op jit(solution)/shard_map/all_gather | solution.py:83
  152.4 4.7 %copy.13 = bf16[16,768,128]{1,2,0:T(8,128)(2,1)} copy(bf16[16,768,128]{2,1,0:T(8,128)(2,1)} %all-gather.2.cloned.1.call-done) | data formatting | bytes 6291456 | tf_op jit(solution)/shard_map/all_gather | solution.py:83
  157.1 2.0 multiply_reduce_fusion
  159.0 0.6 fusion
  159.7 0.0 copy-start.2
  159.7 0.0 copy-start.1
  159.7 3.2 %fusion.11 = bf16[16,24,256]{2,1,0:T(8,128)(2,1)} fusion(bf16[16,768,2,2,32]{1,4,3,2,0:T(8,128)(2,1)} %bitcast.96, f32[16,2,24,768]{3,2,1,0:T(8,128)S(1)} %get-tuple-element.63, f32[16,2,24]{2,1,0:T(2,128)S(1)} %broadcast_maximum_fusion, f32[2]{0:T(128)S(1)} %broadcast_multiply_fusion.2, f32[16,2,24]{2,1,0:T(2,128)S(1)} %fusion, ...), kind=kOutput, calls=%fused_computation.14 | convolution fusion | flops 52248576 | bytes 4167688 | tf_op jit(solution)/shard_map/rhqd,hdc->rqc/dot_general | solution.py:101
  162.9 0.0 all-reduce.3.cloned.1.call-update
  162.9 0.0 all-reduce.5.cloned.1.call-start
  163.0 54.8 %all-reduce.3.cloned.1.call-done = bf16[16,24,256]{2,1,0:T(8,128)(2,1)} async-done(((bf16[16,24,256]{2,1,0:T(8,128)(2,1)}), bf16[16,24,256]{2,1,0:T(8,128)(2,1)}) %all-reduce.3.cloned.1.call-update) | async-done | bytes 196624 | tf_op jit(solution)/shard_map/psum | solution.py:102
  217.8 1.0 fusion.24
  218.8 1.3 collective-permute-start
  220.1 1.3 collective-permute-start.1
  221.5 4.1 %collective-permute-done.1 = bf16[3,24,256]{2,1,0:T(8,128)(2,1)S(1)} collective-permute-done((bf16[3,24,256]{2,1,0:T(8,128)(2,1)S(1)}, bf16[3,24,256]{2,1,0:T(8,128)(2,1)S(1)}, u32[]{:S(2)}, u32[]{:S(2)}) %collective-permute-start.1) | collective-permute-done | bytes 36896 | tf_op jit(solution)/shard_map/ppermute | solution.py:19
  225.6 4.4 %collective-permute-start.2 = (bf16[22,3,256]{2,1,0:T(4,128)(2,1)S(1)}, bf16[22,3,256]{2,1,0:T(4,128)(2,1)S(1)}, u32[]{:S(2)}, u32[]{:S(2)}) collective-permute-start(bf16[22,3,256]{2,1,0:T(4,128)(2,1)S(1)} %get-tuple-element.9), channel_id=1, source_target_pairs={{0,4},{4,8},{8,12},{12,16},{16,20},{20,24},{24,28},{28,32},{32,36}... | collective-permute-start | bytes 101384 | tf_op jit(solution)/shard_map/ppermute | solution.py:18
  230.0 1.9 collective-permute-start.3
  231.9 4.9 %collective-permute-done.3 = bf16[22,3,256]{2,1,0:T(4,128)(2,1)S(1)} collective-permute-done((bf16[22,3,256]{2,1,0:T(4,128)(2,1)S(1)}, bf16[22,3,256]{2,1,0:T(4,128)(2,1)S(1)}, u32[]{:S(2)}, u32[]{:S(2)}) %collective-permute-start.3) | collective-permute-done | bytes 33824 | tf_op jit(solution)/shard_map/ppermute | solution.py:19
  236.8 0.1 maximum_convert_fusion
  237.0 2.9 convert_reduce_fusion.1
  239.9 0.2 fusion.21
  240.2 0.3 fusion.95
  240.5 1.8 convolution_convert_fusion.1
  242.3 0.0 all-reduce.5.cloned.1.call-update
  242.3 59.0 %all-reduce.5.cloned.1.call-done = bf16[16,24,256]{2,1,0:T(8,128)(2,1)} async-done(((bf16[16,24,256]{2,1,0:T(8,128)(2,1)}), bf16[16,24,256]{2,1,0:T(8,128)(2,1)}) %all-reduce.5.cloned.1.call-update) | async-done | bytes 196624 | tf_op jit(solution)/shard_map/psum | solution.py:108
  301.4 1.7 add_convert_fusion
  (33 shorter events, 0.2 us)
Async XLA Ops:
  6.5 233.6 %copy-start = (bf16[256,256]{1,0:T(8,128)(2,1)S(1)}, bf16[256,256]{1,0:T(8,128)(2,1)}, u32[]{:S(2)}) copy-start(bf16[256,256]{1,0:T(8,128)(2,1)} %param.19) | copy-start | bytes 393220
  6.5 5.0 %copy-start.8 = (f32[2]{0:T(128)S(1)}, f32[2]{0:T(128)}, u32[]{:S(2)}) copy-start(f32[2]{0:T(128)} %param.14) | copy-start | bytes 28
  6.5 5.0 %copy-start.3 = (s32[16,256]{1,0:T(8,128)S(1)}, s32[16,256]{1,0:T(8,128)}, u32[]{:S(2)}) copy-start(s32[16,256]{1,0:T(8,128)} %param.16) | copy-start | bytes 49156
  6.5 145.8 %all-gather.2.cloned.1.call-start = ((), (), s32[]{:S(2)}) async-start(), calls=%async_computation | async-start | bytes 3244032 | tf_op jit(solution)/shard_map/all_gather | solution.py:83
  11.5 206.3 %all-reduce.3.cloned.1.call-start = ((), (), s32[]{:S(2)}) async-start(), calls=%async_computation.1 | async-start | bytes 393216 | tf_op jit(solution)/shard_map/psum | solution.py:102
  157.0 2.6 copy-start.6
  159.7 3.3 %copy-start.2 = (bf16[7,7,256]{2,1,0:T(8,128)(2,1)S(1)}, bf16[7,7,256]{2,1,0:T(8,128)(2,1)}, u32[]{:S(2)}) copy-start(bf16[7,7,256]{2,1,0:T(8,128)(2,1)} %param.17) | copy-start | bytes 75268
  159.7 58.2 %copy-start.1 = (bf16[16,24,256]{2,1,0:T(8,128)(2,1)S(1)}, bf16[16,24,256]{2,1,0:T(8,128)(2,1)}, u32[]{:S(2)}) copy-start(bf16[16,24,256]{2,1,0:T(8,128)(2,1)} %param.11) | copy-start | bytes 589828
  162.9 138.5 %all-reduce.5.cloned.1.call-start = ((), (), s32[]{:S(2)}) async-start(), calls=%async_computation.2 | async-start | bytes 393216 | tf_op jit(solution)/shard_map/psum | solution.py:108
  218.8 2.6 collective-permute-start
  220.1 5.4 %collective-permute-start.1 = (bf16[3,24,256]{2,1,0:T(8,128)(2,1)S(1)}, bf16[3,24,256]{2,1,0:T(8,128)(2,1)S(1)}, u32[]{:S(2)}, u32[]{:S(2)}) collective-permute-start(bf16[3,24,256]{2,1,0:T(8,128)(2,1)S(1)} %get-tuple-element.12), channel_id=1, source_target_pairs={{128,0},{256,128},{384,256},{129,1},{257,129},{385,257},{130,2},{2... | collective-permute-start | bytes 110600 | tf_op jit(solution)/shard_map/ppermute | solution.py:19
  225.6 6.3 %collective-permute-start.2 = (bf16[22,3,256]{2,1,0:T(4,128)(2,1)S(1)}, bf16[22,3,256]{2,1,0:T(4,128)(2,1)S(1)}, u32[]{:S(2)}, u32[]{:S(2)}) collective-permute-start(bf16[22,3,256]{2,1,0:T(4,128)(2,1)S(1)} %get-tuple-element.9), channel_id=1, source_target_pairs={{0,4},{4,8},{8,12},{12,16},{16,20},{20,24},{24,28},{28,32},{32,36}... | collective-permute-start | bytes 101384 | tf_op jit(solution)/shard_map/ppermute | solution.py:18
  230.0 6.8 %collective-permute-start.3 = (bf16[22,3,256]{2,1,0:T(4,128)(2,1)S(1)}, bf16[22,3,256]{2,1,0:T(4,128)(2,1)S(1)}, u32[]{:S(2)}, u32[]{:S(2)}) collective-permute-start(bf16[22,3,256]{2,1,0:T(4,128)(2,1)S(1)} %get-tuple-element.10), channel_id=1, source_target_pairs={{4,0},{8,4},{12,8},{16,12},{20,16},{24,20},{28,24},{32,28},{36,32}... | collective-permute-start | bytes 101384 | tf_op jit(solution)/shard_map/ppermute | solution.py:19
  236.9 3.2 %copy-start.7 = (f32[256]{0:T(256)S(1)}, f32[256]{0:T(256)}, u32[]{:S(2)}) copy-start(f32[256]{0:T(256)} %param.18) | copy-start | bytes 3076
  237.0 3.6 %copy-start.5 = (bf16[256,256]{1,0:T(8,128)(2,1)S(1)}, bf16[256,256]{1,0:T(8,128)(2,1)}, u32[]{:S(2)}) copy-start(bf16[256,256]{1,0:T(8,128)(2,1)} %param.20) | copy-start | bytes 393220
  240.5 1.8 copy-start.4
Sparse Core Ops, SparseCore 0:
  11.6 140.6 all-gather.1
  163.0 54.7 all-reduce.2
  242.4 58.8 all-reduce.4
where the time goes:
time: 310 us
  waiting for transfers between devices  264 us (85%)
  between operations  13.4 us (4%)
  starting transfers between devices  8.95 us (3%)
  other arithmetic  8.84 us (3%)
  matrix products  8.69 us (3%)
  local copies, waits for them, and re-layouts  6.01 us (2%)
    all_gather x1, waiting for transfers between devices, shards(): piece = lax.all_gather(keys_values, 'lon', axis=1, tiled=True)  141 us
    psum x1, waiting for transfers between devices, shards(): lax.psum(feed_forward(spatial, norm_gain2, w_up, w_down).astype(jnp.bfloa...  59 us
    psum x1, waiting for transfers between devices, shards(): lax.psum(partial_value.astype(jnp.bfloat16), 'tensor').astype(jnp.float32)  54.8 us
    ppermute x2, waiting for transfers between devices, padded(): after = lax.ppermute(first, axis, down)  8.96 us
  transfers between devices with their start and end apart: 7, of which 5 were waited for; matrix products, arithmetic and copies ran while one was open for 0% of the time, Pallas kernels for 0%

commit v1 on v0

--- a/solution.py
+++ b/solution.py
@@ -80,7 +80,15 @@
     ).astype(jnp.bfloat16)
     queries = projected[:, :, 0]
     keys_values = projected[:, :, 1:].reshape(lat_rows, lon_cols, 2 * local_heads * head_size)
-    piece = lax.all_gather(keys_values, "lon", axis=1, tiled=True)
+    piece = jnp.concatenate(
+        lax.all_to_all(
+            jnp.stack([keys_values for _ in range(lax.axis_size("lon"))]),
+            axis_name="lon",
+            concat_axis=0,
+            split_axis=0,
+        ),
+        axis=1,
+    )
     running_max = jnp.full((lat_rows, local_heads, lon_cols), -1e30, jnp.float32)
     count = piece.shape[1]
     split_piece = piece.reshape(lat_rows, count, 2, local_heads, head_size)

time: 310 us -> 393 us (1.27)
  local copies, waits for them, and re-layouts: 6.01 us -> 73.5 us
  starting transfers between devices: 8.95 us -> 25.8 us
    all_to_all x0 -> x1, waiting for transfers between devices: none -> 145 us  [shards(): lax.all_to_all(jnp.stack([keys_values for _ in range(lax.axis_size('lon')...]
    all_gather x1 -> x0, waiting for transfers between devices: 141 us -> none  [shards(): piece = lax.all_gather(keys_values, 'lon', axis=1, tiled=True)]
    unnamed x18 -> x22, local copies, waits for them, and re-layouts: 0.05 us -> 30.8 us
    another operation x0 -> x3, local copies, waits for them, and re-layouts: none -> 28.1 us  [the longest x1 25.6 us: shards(): split_piece = piece.reshape(lat_rows, count, 2, local_heads, head_size)]
    all_to_all x0 -> x1, starting transfers between devices: none -> 16.8 us  [shards(): lax.all_to_all(jnp.stack([keys_values for _ in range(lax.axis_size('lon')...]
    slice x0 -> x1, local copies, waits for them, and re-layouts: none -> 11.6 us  [shards(): split_piece[:, :, 0]]
    psum x1, waiting for transfers between devices: 54.8 us -> 48.1 us  [shards(): lax.psum(partial_value.astype(jnp.bfloat16), 'tensor').astype(jnp.float32)]
    all_gather x1 -> x0, local copies, waits for them, and re-layouts: 4.69 us -> none  [shards(): piece = lax.all_gather(keys_values, 'lon', axis=1, tiled=True)]
where the time goes in v1:
time: 393 us; the launch traced here: 392 us
  waiting for transfers between devices  261 us (66%)
  local copies, waits for them, and re-layouts  73.5 us (19%)
  starting transfers between devices  25.8 us (7%)
  between operations  13.7 us (3%)
  other arithmetic  8.84 us (2%)
  matrix products  8.79 us (2%)
    all_to_all x1, waiting for transfers between devices, shards(): lax.all_to_all(jnp.stack([keys_values for _ in range(lax.axis_size('lon')...  145 us
    psum x1, waiting for transfers between devices, shards(): lax.psum(feed_forward(spatial, norm_gain2, w_up, w_down).astype(jnp.bfloa...  59 us
    psum x1, waiting for transfers between devices, shards(): lax.psum(partial_value.astype(jnp.bfloat16), 'tensor').astype(jnp.float32)  48.1 us
    unnamed x22, local copies, waits for them, and re-layouts  30.8 us
    another operation x1, local copies, waits for them, and re-layouts, shards(): split_piece = piece.reshape(lat_rows, count, 2, local_heads, head_size)  25.6 us
    all_to_all x1, starting transfers between devices, shards(): lax.all_to_all(jnp.stack([keys_values for _ in range(lax.axis_size('lon')...  16.8 us
    slice x1, local copies, waits for them, and re-layouts, shards(): split_piece[:, :, 0]  11.6 us
    ppermute x2, waiting for transfers between devices, padded(): after = lax.ppermute(first, axis, down)  8.96 us
  transfers between devices with their start and end apart: 7, of which 5 were waited for; matrix products, arithmetic and copies ran while one was open for 0% of the time, Pallas kernels for 0%

profile of v1, /device:TPU:2, one launch (start us, length us, event | category | flops | bytes accessed | tf_op | source)
XLA Modules:
  0.0 391.9 jit_solution(2880584676956770868)
XLA Ops:
  6.5 1.1 convert_reduce_fusion
  7.6 1.2 fusion.26
  8.8 1.4 convolution_convert_fusion
  10.2 0.9 copy-done.2
  11.2 0.3 copy.14
  11.5 0.2 stack_reshape.2
  11.7 2.4 stack.3
  14.1 16.8 %all-to-all-start = ((bf16[32,16,24,128]{3,2,1,0:T(8,128)(2,1)}), bf16[32,16,24,128]{3,2,1,0:T(8,128)(2,1)S(1)}, u32[]{:S(2)}, u32[]{:S(2)}) async-start(bf16[32,16,24,128]{3,2,1,0:T(8,128)(2,1)} %stack.3), calls=%async_computation | async-start | bytes 6291456 | tf_op jit(solution)/shard_map/all_to_all | solution.py:84
  31.0 145.2 %all-to-all-done = bf16[32,16,24,128]{3,2,1,0:T(8,128)(2,1)S(1)} async-done(((bf16[32,16,24,128]{3,2,1,0:T(8,128)(2,1)}), bf16[32,16,24,128]{3,2,1,0:T(8,128)(2,1)S(1)}, u32[]{:S(2)}, u32[]{:S(2)}) %all-to-all-start) | async-done | bytes 3145760 | tf_op jit(solution)/shard_map/all_to_all | solution.py:84
  176.2 2.5 copy.15
  178.7 25.6 %reshape_reshape.3 = bf16[16,768,2,2,32]{4,3,2,1,0:T(2,128)(2,1)} reshape(bf16[16,32,24,128]{3,2,1,0:T(8,128)(2,1)} %copy.15) | data formatting | bytes 6291456 | tf_op jit(solution)/shard_map/reshape;reshape | solution.py:94
  204.2 11.6 %fusion.143 = (bf16[16,768,1,2,32]{4,3,2,1,0:T(2,128)(2,1)}, bf16[16,768,1,2,32]{4,3,2,1,0:T(2,128)(2,1)}) fusion(bf16[16,768,2,2,32]{4,3,2,1,0:T(2,128)(2,1)} %reshape_reshape.3), kind=kLoop, calls=%fused_computation.214 | loop fusion | bytes 6291456 | tf_op jit(solution)/shard_map/slice | solution.py:96
  215.8 14.9 %copy.20 = bf16[16,768,1,2,32]{1,4,3,0,2:T(8,128)(2,1)} copy(bf16[16,768,1,2,32]{4,3,2,1,0:T(2,128)(2,1)} %get-tuple-element.9) | data formatting | bytes 3145728
  230.7 2.1 multiply_reduce_fusion
  232.8 14.9 %copy.21 = bf16[16,768,1,2,32]{1,4,3,0,2:T(8,128)(2,1)} copy(bf16[16,768,1,2,32]{4,3,2,1,0:T(2,128)(2,1)} %get-tuple-element.10) | data formatting | bytes 3145728
  247.7 0.6 fusion
  248.3 0.2 copy-done.7
  248.5 3.2 fusion.17
  251.8 48.1 %all-reduce.3.cloned.1.call-done = bf16[16,24,256]{2,1,0:T(8,128)(2,1)} async-done(((bf16[16,24,256]{2,1,0:T(8,128)(2,1)}), bf16[16,24,256]{2,1,0:T(8,128)(2,1)}) %all-reduce.3.cloned.1.call-update) | async-done | bytes 196624 | tf_op jit(solution)/shard_map/psum | solution.py:110
  299.9 1.0 fusion.32
  300.9 1.3 collective-permute-start
  302.2 1.3 collective-permute-start.1
  303.5 4.1 %collective-permute-done.1 = bf16[3,24,256]{2,1,0:T(8,128)(2,1)S(1)} collective-permute-done((bf16[3,24,256]{2,1,0:T(8,128)(2,1)S(1)}, bf16[3,24,256]{2,1,0:T(8,128)(2,1)S(1)}, u32[]{:S(2)}, u32[]{:S(2)}) %collective-permute-start.1) | collective-permute-done | bytes 36896 | tf_op jit(solution)/shard_map/ppermute | solution.py:19
  307.7 4.4 %collective-permute-start.2 = (bf16[22,3,256]{2,1,0:T(4,128)(2,1)S(1)}, bf16[22,3,256]{2,1,0:T(4,128)(2,1)S(1)}, u32[]{:S(2)}, u32[]{:S(2)}) collective-permute-start(bf16[22,3,256]{2,1,0:T(4,128)(2,1)S(1)} %get-tuple-element.11), channel_id=1, source_target_pairs={{0,4},{4,8},{8,12},{12,16},{16,20},{20,24},{24,28},{28,32},{32,36}... | collective-permute-start | bytes 101384 | tf_op jit(solution)/shard_map/ppermute | solution.py:18
  312.0 1.9 collective-permute-start.3
  314.0 4.9 %collective-permute-done.3 = bf16[22,3,256]{2,1,0:T(4,128)(2,1)S(1)} collective-permute-done((bf16[22,3,256]{2,1,0:T(4,128)(2,1)S(1)}, bf16[22,3,256]{2,1,0:T(4,128)(2,1)S(1)}, u32[]{:S(2)}, u32[]{:S(2)}) %collective-permute-start.3) | collective-permute-done | bytes 33824 | tf_op jit(solution)/shard_map/ppermute | solution.py:19
  319.0 2.9 convert_reduce_fusion.1
  322.0 0.2 fusion.29
  322.2 0.3 fusion.103
  322.6 1.8 convolution_convert_fusion.1
  324.4 59.0 %all-reduce.5.cloned.1.call-done = bf16[16,24,256]{2,1,0:T(8,128)(2,1)} async-done(((bf16[16,24,256]{2,1,0:T(8,128)(2,1)}), bf16[16,24,256]{2,1,0:T(8,128)(2,1)}) %all-reduce.5.cloned.1.call-update) | async-done | bytes 196624 | tf_op jit(solution)/shard_map/psum | solution.py:116
  383.4 1.7 add_convert_fusion
  (39 shorter events, 0.5 us)
Async XLA Ops:
  6.5 315.7 %copy-start = (bf16[256,256]{1,0:T(8,128)(2,1)S(1)}, bf16[256,256]{1,0:T(8,128)(2,1)}, u32[]{:S(2)}) copy-start(bf16[256,256]{1,0:T(8,128)(2,1)} %param.19) | copy-start | bytes 393220
  10.2 0.9 copy-start.2
  14.1 16.9 %copy-start.9 = (f32[2]{0:T(128)S(1)}, f32[2]{0:T(128)}, u32[]{:S(2)}) copy-start(f32[2]{0:T(128)} %param.14) | copy-start | bytes 28
  14.1 16.9 %copy-start.4 = (s32[16,256]{1,0:T(8,128)S(1)}, s32[16,256]{1,0:T(8,128)}, u32[]{:S(2)}) copy-start(s32[16,256]{1,0:T(8,128)} %param.16) | copy-start | bytes 49156
  14.1 162.1 %all-to-all-start = ((bf16[32,16,24,128]{3,2,1,0:T(8,128)(2,1)}), bf16[32,16,24,128]{3,2,1,0:T(8,128)(2,1)S(1)}, u32[]{:S(2)}, u32[]{:S(2)}) async-start(bf16[32,16,24,128]{3,2,1,0:T(8,128)(2,1)} %stack.3), calls=%async_computation | async-start | bytes 6291456 | tf_op jit(solution)/shard_map/all_to_all | solution.py:84
  30.9 269.0 %all-reduce.3.cloned.1.call-start = ((), (), s32[]{:S(2)}) async-start(), calls=%async_computation.1 | async-start | bytes 393216 | tf_op jit(solution)/shard_map/psum | solution.py:110
  247.7 0.8 copy-start.7
  248.5 3.3 copy-start.3
  248.5 51.4 %copy-start.1 = (bf16[16,24,256]{2,1,0:T(8,128)(2,1)S(1)}, bf16[16,24,256]{2,1,0:T(8,128)(2,1)}, u32[]{:S(2)}) copy-start(bf16[16,24,256]{2,1,0:T(8,128)(2,1)} %param.11) | copy-start | bytes 589828
  251.7 131.7 %all-reduce.5.cloned.1.call-start = ((), (), s32[]{:S(2)}) async-start(), calls=%async_computation.2 | async-start | bytes 393216 | tf_op jit(solution)/shard_map/psum | solution.py:116
  300.9 2.6 collective-permute-start
  302.2 5.4 %collective-permute-start.1 = (bf16[3,24,256]{2,1,0:T(8,128)(2,1)S(1)}, bf16[3,24,256]{2,1,0:T(8,128)(2,1)S(1)}, u32[]{:S(2)}, u32[]{:S(2)}) collective-permute-start(bf16[3,24,256]{2,1,0:T(8,128)(2,1)S(1)} %get-tuple-element.14), channel_id=1, source_target_pairs={{128,0},{256,128},{384,256},{129,1},{257,129},{385,257},{130,2},{2... | collective-permute-start | bytes 110600 | tf_op jit(solution)/shard_map/ppermute | solution.py:19
  307.7 6.3 %collective-permute-start.2 = (bf16[22,3,256]{2,1,0:T(4,128)(2,1)S(1)}, bf16[22,3,256]{2,1,0:T(4,128)(2,1)S(1)}, u32[]{:S(2)}, u32[]{:S(2)}) collective-permute-start(bf16[22,3,256]{2,1,0:T(4,128)(2,1)S(1)} %get-tuple-element.11), channel_id=1, source_target_pairs={{0,4},{4,8},{8,12},{12,16},{16,20},{20,24},{24,28},{28,32},{32,36}... | collective-permute-start | bytes 101384 | tf_op jit(solution)/shard_map/ppermute | solution.py:18
  312.0 6.8 %collective-permute-start.3 = (bf16[22,3,256]{2,1,0:T(4,128)(2,1)S(1)}, bf16[22,3,256]{2,1,0:T(4,128)(2,1)S(1)}, u32[]{:S(2)}, u32[]{:S(2)}) collective-permute-start(bf16[22,3,256]{2,1,0:T(4,128)(2,1)S(1)} %get-tuple-element.12), channel_id=1, source_target_pairs={{4,0},{8,4},{12,8},{16,12},{20,16},{24,20},{28,24},{32,28},{36,32}... | collective-permute-start | bytes 101384 | tf_op jit(solution)/shard_map/ppermute | solution.py:19
  319.0 3.2 copy-start.8
  319.0 3.6 copy-start.6
  322.6 1.8 copy-start.5
Sparse Core Ops, SparseCore 0:
  251.8 48.0 all-reduce.2
  324.5 58.8 all-reduce.4
